TPU v7x, 256 devices: a whole 4x4x8 slice. The times are simulated.
256 devices in a mesh: dp: 32 (over z, x), tensor: 8 (over y, core).
Axes of the slice: x: 4, y: 4, z: 8, core: 2. Of those that a mesh axis runs over, the one named last changes fastest.
Arguments:
- tokens: bfloat16 [65536, 8192], P('dp', 'tensor'), may hold values from -6 to 6
- base_value_weight: bfloat16 [8192, 1024], P('tensor'), may hold values from -0.0625 to 0.0625
- adapter_down_weight: bfloat16 [512, 8192, 64], P('dp', 'tensor'), may hold values from -0.0625 to 0.0625
- adapter_up_weight: bfloat16 [512, 64, 1024], P('dp', None, 'tensor'), may hold values from -0.75 to 0.75
- request_adapter_index: int32 [128], P('dp'), may hold values from 0 to 511
- storage_index_table: int32 [512], replicated, may hold values from 0 to 511, each once
Outputs:
- values_out: bfloat16 [65536, 1024], P('dp', 'tensor')
Inputs may be any that keep to these rules, and one draw needn't show every extreme that they name: `request_adapter_index`: each adapter id names an adapter. storage_index_table is a permutation of the storage positions.
All inputs are finite; a program needn't handle non-finite values.
Results may differ from a plain program's by a relative error of at most 0.003.
Values may be sent and summed in bfloat16 or wider, within the bound.
A program may use at most 128 MiB of HBM per device.

v0:
```python
import jax
import jax.numpy as jnp
from jax import lax
from jax.sharding import PartitionSpec as P

adapter_scale = 0.5


def shards(
    tokens,
    base_value_weight,
    adapter_down_weight,
    adapter_up_weight,
    request_adapter_index,
    storage_index_table,
):
    n_rows, width = tokens.shape
    requests_here = request_adapter_index.shape[0]
    seq_len = n_rows // requests_here
    owned_columns = adapter_down_weight.shape[0]
    adapter_rank_size = adapter_down_weight.shape[2]
    local_columns = adapter_up_weight.shape[2]
    all_adapters = storage_index_table.shape[0]
    down_width = width * adapter_rank_size
    base_projection = lax.psum_scatter(
        lax.dot_general(
            base_value_weight, tokens, (((0,), (1,)), ((), ())), preferred_element_type=jnp.float32
        ),
        "tensor",
        scatter_dimension=0,
        tiled=True,
    ).T
    every_id = lax.all_gather(request_adapter_index, "dp", axis=0, tiled=True)
    catalog = lax.broadcasted_iota(jnp.int32, (every_id.shape[0], all_adapters), 1)
    picked = (every_id[:, None] == catalog).astype(jnp.int32)
    positions = jnp.sum(picked * storage_index_table[None, :], axis=1)
    local_place = positions - lax.axis_index("dp") * owned_columns
    owner_slots = lax.broadcasted_iota(jnp.int32, (every_id.shape[0], owned_columns), 1)
    match = (local_place[:, None] == owner_slots).astype(jnp.bfloat16)
    panels = jnp.concatenate(
        (
            adapter_down_weight.reshape(owned_columns, down_width),
            adapter_up_weight.reshape(owned_columns, adapter_rank_size * local_columns),
        ),
        axis=1,
    )
    outgoing = jnp.dot(match, panels, preferred_element_type=jnp.bfloat16)
    outgoing = outgoing.reshape(lax.axis_size("dp"), requests_here, panels.shape[1])
    fetched = jnp.sum(
        lax.all_to_all(outgoing, "dp", split_axis=0, concat_axis=0, tiled=True), axis=0
    )
    down_sel = fetched[:, :down_width].reshape(requests_here, width, adapter_rank_size)
    up_sel = fetched[:, down_width:].reshape(requests_here, adapter_rank_size, local_columns)
    grouped = tokens.reshape(requests_here, seq_len, width)
    low_part = jnp.einsum("rsd,rdk->rsk", grouped, down_sel, preferred_element_type=jnp.float32)
    low = lax.psum(low_part, "tensor").astype(jnp.bfloat16)
    adapter_update = jnp.einsum("rsk,rkc->rsc", low, up_sel, preferred_element_type=jnp.float32)
    adapter_update = adapter_update.reshape(n_rows, local_columns)
    return (base_projection + adapter_scale * adapter_update).astype(jnp.bfloat16)


def solution(mesh):
    return jax.shard_map(
        shards,
        mesh=mesh,
        in_specs=(
            P("dp", "tensor"),
            P("tensor", None),
            P("dp", "tensor", None),
            P("dp", None, "tensor"),
            P("dp"),
            P(),
        ),
        out_specs=P("dp", "tensor"),
        check_vma=False,
    )
```

profile of v0, /device:TPU:102, one launch (start us, length us, event | category | flops | bytes accessed | tf_op | source)
XLA Modules:
  0.0 573.9 jit_solution(4957867999160425157)
XLA Ops:
  6.5 0.0 copy-start
  6.5 1.4 dynamic-slice
  8.6 0.9 dynamic-update-slice
  9.5 19.0 %all-reduce = s32[128]{0:T(128)S(1)} all-reduce(s32[128]{0:T(128)S(1)} %dynamic-update-slice), channel_id=1, replica_groups=mesh['dp'=32,'tensor'=8] {'dp'}, use_global_device_ids=true, to_apply=%add | all-reduce | flops 128 | bytes 1024
  28.5 4.8 copy.12
  33.3 0.0 copy-start.2
  33.3 5.8 %reshape.26 = bf16[16,65536]{1,0:T(8,128)(2,1)} reshape(bf16[16,1024,64]{2,1,0:T(8,128)(2,1)} %copy.12) | data formatting | bytes 4194304 | tf_op jit(solution)/shard_map/reshape | solution.py:42
  39.0 0.0 copy-done.2
  39.0 0.2 copy.25
  39.2 0.0 copy-done.3
  39.2 0.2 select_reduce_fusion
  39.4 10.7 %fusion = bf16[128,73728]{1,0:T(8,128)(2,1)} fusion(bf16[16,8192]{1,0:T(8,128)(2,1)S(1)} %bitcast.25, bf16[16,65536]{1,0:T(8,128)(2,1)} %reshape.26, s32[128]{0:T(128)S(1)} %broadcast_subtract_fusion), kind=kOutput, calls=%fused_computation | convolution fusion | flops 306710528 | bytes 21234176 | tf_op jit(solution)/shard_map/dot_general | solution.py:47
  50.1 21.1 %reshape.28 = bf16[32,4,73728]{2,1,0:T(4,128)(2,1)} reshape(bf16[128,73728]{1,0:T(8,128)(2,1)} %fusion) | data formatting | bytes 37748736 | tf_op jit(solution)/shard_map/reshape | solution.py:48
  71.2 8.3 %all-to-all-start = ((bf16[32,4,73728]{2,1,0:T(4,128)(2,1)}), bf16[32,4,73728]{2,1,0:T(4,128)(2,1)}, u32[]{:S(2)}, u32[]{:S(2)}) async-start(bf16[32,4,73728]{2,1,0:T(4,128)(2,1)} %reshape.28), calls=%async_computation.1 | async-start | bytes 37748736 | tf_op jit(solution)/shard_map/all_to_all | solution.py:50
  79.5 0.0 reduce-scatter.2.cloned.1.call-start
  79.6 0.0 copy-done
  79.6 8.9 %fusion.10 = f32[1024,2048]{1,0:T(8,128)} fusion(bf16[1024,1024]{1,0:T(8,128)(2,1)S(1)} %copy-done, bf16[2048,1024]{1,0:T(8,128)(2,1)} %param.6), kind=kOutput, calls=%fused_computation.19 | convolution fusion | flops 4294967296 | bytes 14680064 | tf_op jit(solution)/shard_map/dot_general | solution.py:26
  88.5 0.0 reduce-scatter.2.cloned.1.call-update
  88.6 423.3 %all-to-all-done = bf16[32,4,73728]{2,1,0:T(4,128)(2,1)} async-done(((bf16[32,4,73728]{2,1,0:T(4,128)(2,1)}), bf16[32,4,73728]{2,1,0:T(4,128)(2,1)}, u32[]{:S(2)}, u32[]{:S(2)}) %all-to-all-start) | async-done | bytes 18874400 | tf_op jit(solution)/shard_map/all_to_all | solution.py:50
  511.9 9.3 %reduce_sum.22 = bf16[4,73728]{1,0:T(4,128)(2,1)S(1)} reduce(bf16[32,4,73728]{2,1,0:T(4,128)(2,1)} %all-to-all-done, bf16[]{:T(256)} %constant.14.clone.1), dimensions={0}, to_apply=%region_2.0 | reduce | flops 9142272 | bytes 19464194 | tf_op jit(solution)/shard_map/reduce_sum | solution.py:49
  521.2 0.0 copy-start.1
  521.2 0.8 copy-done.1
  522.0 1.0 slice.8
  523.0 1.9 reshape.29
  524.9 4.4 convolution_bitcast_fusion
  529.3 0.9 slice_bitcast_fusion
  530.2 29.8 %all-reduce.2 = bf16[4,512,64]{1,2,0:T(8,128)(2,1)S(1)} all-reduce(f32[4,512,64]{1,2,0:T(8,128)} %convolution_bitcast_fusion), channel_id=1, replica_groups=mesh['dp'=32,'tensor'=8] {'tensor'}, use_global_device_ids=true, to_apply=%region_3.0 | all-reduce | flops 131072 | bytes 786432 | tf_op jit(solution)/shard_map/psum | solution.py:56
  560.0 1.3 convolution_multiply_fusion
  561.3 1.6 copy.17
  562.9 0.0 reduce-scatter.2.cloned.1.call-done
  562.9 2.1 fusion.4
  565.0 2.0 copy.15
  (3 shorter events, 0.0 us)
Async XLA Ops:
  6.5 73.1 %copy-start = (bf16[1024,1024]{1,0:T(8,128)(2,1)S(1)}, bf16[1024,1024]{1,0:T(8,128)(2,1)}, u32[]{:S(2)}) copy-start(bf16[1024,1024]{1,0:T(8,128)(2,1)} %param.7) | copy-start | bytes 6291460
  33.3 5.8 %copy-start.2 = (bf16[16,64,128]{2,1,0:T(8,128)(2,1)S(1)}, bf16[16,64,128]{2,1,0:T(8,128)(2,1)}, u32[]{:S(2)}) copy-start(bf16[16,64,128]{2,1,0:T(8,128)(2,1)} %param.9) | copy-start | bytes 786436
  33.3 5.9 %copy-start.3 = (s32[512]{0:T(512)S(1)}, s32[512]{0:T(512)}, u32[]{:S(2)}) copy-start(s32[512]{0:T(512)} %param.11) | copy-start | bytes 6148
  71.2 440.7 %all-to-all-start = ((bf16[32,4,73728]{2,1,0:T(4,128)(2,1)}), bf16[32,4,73728]{2,1,0:T(4,128)(2,1)}, u32[]{:S(2)}, u32[]{:S(2)}) async-start(bf16[32,4,73728]{2,1,0:T(4,128)(2,1)} %reshape.28), calls=%async_computation.1 | async-start | bytes 37748736 | tf_op jit(solution)/shard_map/all_to_all | solution.py:50
  79.5 483.3 %reduce-scatter.2.cloned.1.call-start = ((), (), s32[]{:S(2)}) async-start(), calls=%async_computation.2 | async-start | bytes 9437184 | tf_op jit(solution)/shard_map/reduce_scatter | solution.py:25
  521.2 0.8 copy-start.1
Sparse Core Ops, SparseCore 0:
  88.7 56.3 reduce-scatter.1
where the time goes:
time: 575 us; the launch traced here: 574 us
  waiting for transfers between devices  423 us (74%)
  blocking collectives  48.8 us (8%)
  local copies, waits for them, and re-layouts  42.2 us (7%)
  matrix products  25.4 us (4%)
  between operations  14.2 us (2%)
  other arithmetic  11.6 us (2%)
  starting transfers between devices  8.39 us (1%)
    all_to_all x1, waiting for transfers between devices, shards(): lax.all_to_all(outgoing, 'dp', split_axis=0, concat_axis=0, tiled=True)  423 us
    psum x1, blocking collectives, shards(): low = lax.psum(low_part, 'tensor').astype(jnp.bfloat16)  29.8 us
    reshape x1, local copies, waits for them, and re-layouts, shards(): outgoing.reshape(lax.axis_size('dp'), requests_here, panels.shape[1])  21.1 us
    unnamed x1, blocking collectives  19 us
  transfers between devices with their start and end apart: 2, of which 1 were waited for; matrix products, arithmetic and copies ran while one was open for 5% of the time, Pallas kernels for 0%

commit v1 on v0

--- a/solution.py
+++ b/solution.py
@@ -2,6 +2,7 @@
 import jax.numpy as jnp
 from jax import lax
 from jax.sharding import PartitionSpec as P
+from jax.lax import all_gather
 
 adapter_scale = 0.5
 
@@ -53,7 +54,7 @@
     up_sel = fetched[:, down_width:].reshape(requests_here, adapter_rank_size, local_columns)
     grouped = tokens.reshape(requests_here, seq_len, width)
     low_part = jnp.einsum("rsd,rdk->rsk", grouped, down_sel, preferred_element_type=jnp.float32)
-    low = lax.psum(low_part, "tensor").astype(jnp.bfloat16)
+    low = jnp.sum(all_gather(low_part, "tensor"), axis=0).astype(jnp.bfloat16)
     adapter_update = jnp.einsum("rsk,rkc->rsc", low, up_sel, preferred_element_type=jnp.float32)
     adapter_update = adapter_update.reshape(n_rows, local_columns)
     return (base_projection + adapter_scale * adapter_update).astype(jnp.bfloat16)

time: 575 us -> 606 us (1.054)
  blocking collectives: 48.8 us -> 431 us
  waiting for transfers between devices: 423 us -> 76.5 us
  starting transfers between devices: 8.39 us -> 0.22 us
    all_to_all x1 -> x0, waiting for transfers between devices: 423 us -> none  [shards(): lax.all_to_all(outgoing, 'dp', split_axis=0, concat_axis=0, tiled=True)]
    all_to_all x0 -> x1, blocking collectives: none -> 412 us  [shards(): lax.all_to_all(outgoing, 'dp', split_axis=0, concat_axis=0, tiled=True)]
    reduce_scatter x1, waiting for transfers between devices: 0.02 us -> 51.9 us  [shards(): lax.psum_scatter(lax.dot_general(base_value_weight, tokens, (((0,), (1,))...]
    psum x1 -> x0, blocking collectives: 29.8 us -> none  [shards(): low = lax.psum(low_part, 'tensor').astype(jnp.bfloat16)]
    all_gather x0 -> x1, waiting for transfers between devices: none -> 24.6 us  [shards(): low = jnp.sum(all_gather(low_part, 'tensor'), axis=0).astype(jnp.bfloat16)]
    all_to_all x1 -> x0, starting transfers between devices: 8.34 us -> none  [shards(): lax.all_to_all(outgoing, 'dp', split_axis=0, concat_axis=0, tiled=True)]
  transfers between devices with their start and end apart: 2 -> 2, of which waited for: 1 -> 2; matrix products, arithmetic and copies ran while one was open for 5% -> 3% of each run, Pallas kernels for 0% -> 0%
where the time goes in v1:
time: 606 us; the launch traced here: 603 us
  blocking collectives  431 us (71%)
  waiting for transfers between devices  76.5 us (13%)
  local copies, waits for them, and re-layouts  42.1 us (7%)
  matrix products  25.5 us (4%)
  other arithmetic  14.3 us (2%)
  between operations  14.1 us (2%)
    all_to_all x1, blocking collectives, shards(): lax.all_to_all(outgoing, 'dp', split_axis=0, concat_axis=0, tiled=True)  412 us
    reduce_scatter x1, waiting for transfers between devices, shards(): lax.psum_scatter(lax.dot_general(base_value_weight, tokens, (((0,), (1,))...  51.9 us
    all_gather x1, waiting for transfers between devices, shards(): low = jnp.sum(all_gather(low_part, 'tensor'), axis=0).astype(jnp.bfloat16)  24.6 us
    reshape x1, local copies, waits for them, and re-layouts, shards(): outgoing.reshape(lax.axis_size('dp'), requests_here, panels.shape[1])  21 us
    unnamed x1, blocking collectives  19 us
  transfers between devices with their start and end apart: 2, of which 2 were waited for; matrix products, arithmetic and copies ran while one was open for 3% of the time, Pallas kernels for 0%

profile of v1, /device:TPU:102, one launch (start us, length us, event | category | flops | bytes accessed | tf_op | source)
XLA Modules:
  0.0 603.5 jit_solution(4029210360239520753)
XLA Ops:
  6.5 0.0 copy-start
  6.5 0.0 all-gather.3.cloned.1.call-start
  6.5 1.4 dynamic-slice
  8.6 0.9 dynamic-update-slice
  9.5 19.0 %all-reduce = s32[128]{0:T(128)S(1)} all-reduce(s32[128]{0:T(128)S(1)} %dynamic-update-slice), channel_id=1, replica_groups=mesh['dp'=32,'tensor'=8] {'dp'}, use_global_device_ids=true, to_apply=%add | all-reduce | flops 128 | bytes 1024
  28.5 4.8 copy.17
  33.3 5.7 reshape.26
  39.0 0.0 copy-done.2
  39.0 0.2 copy.30
  39.2 0.2 select_reduce_fusion
  39.4 10.7 %fusion = bf16[128,73728]{1,0:T(8,128)(2,1)} fusion(bf16[16,8192]{1,0:T(8,128)(2,1)S(1)} %bitcast.27, bf16[16,65536]{1,0:T(8,128)(2,1)} %reshape.26, s32[128]{0:T(128)S(1)} %broadcast_subtract_fusion), kind=kOutput, calls=%fused_computation | convolution fusion | flops 306710528 | bytes 21234176 | tf_op jit(solution)/shard_map/dot_general | solution.py:48
  50.1 21.0 %reshape.28 = bf16[32,4,73728]{2,1,0:T(4,128)(2,1)} reshape(bf16[128,73728]{1,0:T(8,128)(2,1)} %fusion) | data formatting | bytes 37748736 | tf_op jit(solution)/shard_map/reshape | solution.py:49
  71.1 411.6 %all_to_all.5 = bf16[32,4,73728]{2,1,0:T(4,128)(2,1)} all-to-all(bf16[32,4,73728]{2,1,0:T(4,128)(2,1)} %reshape.28), channel_id=1, replica_groups=mesh['dp'=32,'tensor'=8] {'dp'}, dimensions={0} | all-to-all | bytes 37748736 | tf_op jit(solution)/shard_map/all_to_all | solution.py:51
  482.8 9.3 %reduce_sum.31 = bf16[4,73728]{1,0:T(4,128)(2,1)S(1)} reduce(bf16[32,4,73728]{2,1,0:T(4,128)(2,1)} %all_to_all.5, bf16[]{:T(256)} %constant.14.clone.1), dimensions={0}, to_apply=%region_2.0 | reduce | flops 9142272 | bytes 19464194 | tf_op jit(solution)/shard_map/reduce_sum | solution.py:50
  492.1 0.0 copy-start.1
  492.1 0.8 copy-done.1
  492.9 1.0 slice.8
  493.9 1.9 reshape.29
  495.8 4.4 convolution_bitcast_fusion
  500.2 0.0 all-gather.3.cloned.1.call-update
  500.2 0.2 reduce-scatter.2.cloned.1.call-start
  500.4 0.0 copy-done
  500.4 9.0 %fusion.10 = f32[1024,2048]{1,0:T(8,128)} fusion(bf16[1024,1024]{1,0:T(8,128)(2,1)S(1)} %copy-done, bf16[2048,1024]{1,0:T(8,128)(2,1)} %param.6), kind=kOutput, calls=%fused_computation.19 | convolution fusion | flops 4294967296 | bytes 14680064 | tf_op jit(solution)/shard_map/dot_general | solution.py:27
  509.4 0.0 reduce-scatter.2.cloned.1.call-update
  509.5 0.9 slice_bitcast_fusion
  510.3 24.6 %all-gather.3.cloned.1.call-done = f32[32,512,64]{1,2,0:T(8,128)} async-done(((f32[4,512,64]{1,2,0:T(8,128)}), f32[32,512,64]{1,2,0:T(8,128)}) %all-gather.3.cloned.1.call-update) | async-done | bytes 4194320 | tf_op jit(solution)/shard_map/all_gather | solution.py:57
  534.9 2.7 reduce_sum.32
  537.6 1.4 convolution_multiply_fusion
  539.0 1.6 copy.22
  540.6 51.9 %reduce-scatter.2.cloned.1.call-done = f32[128,2048]{1,0:T(8,128)} async-done(((f32[1024,2048]{1,0:T(8,128)}), f32[128,2048]{1,0:T(8,128)}) %reduce-scatter.2.cloned.1.call-update) | async-done | bytes 1048592 | tf_op jit(solution)/shard_map/reduce_scatter | solution.py:26
  592.5 2.1 fusion.4
  594.6 2.0 copy.20
  (5 shorter events, 0.0 us)
Async XLA Ops:
  6.5 493.9 %copy-start = (bf16[1024,1024]{1,0:T(8,128)(2,1)S(1)}, bf16[1024,1024]{1,0:T(8,128)(2,1)}, u32[]{:S(2)}) copy-start(bf16[1024,1024]{1,0:T(8,128)(2,1)} %param.7) | copy-start | bytes 6291460
  6.5 528.4 %all-gather.3.cloned.1.call-start = ((), (), s32[]{:S(2)}) async-start(), calls=%async_computation.3 | async-start | bytes 4718592 | tf_op jit(solution)/shard_map/all_gather | solution.py:57
  33.3 5.7 copy-start.2
  33.3 5.9 copy-start.3
  492.1 0.8 copy-start.1
  500.2 92.3 %reduce-scatter.2.cloned.1.call-start = ((), (), s32[]{:S(2)}) async-start(), calls=%async_computation.2 | async-start | bytes 9437184 | tf_op jit(solution)/shard_map/reduce_scatter | solution.py:26
Sparse Core Ops, SparseCore 0:
  500.3 34.5 all-gather.2
  537.5 54.9 reduce-scatter.1
